TPU v7x, 128 devices: a whole 4x4x4 slice. The times are simulated.
128 devices in a mesh: cam: 4 (over z_hi, core), lmk: 32 (over y, z_lo, x).
Axes of the slice: x: 4, y: 4, z: 4 (z_hi: 2, z_lo: 2; z = z_hi * 2 + z_lo), core: 2. Of those that a mesh axis runs over, the one named last changes fastest.
Arguments:
- probes: bfloat16 [128, 32, 576], P(('cam', 'lmk')), may hold values from -6 to 6
- u_inverse: bfloat16 [128, 576, 576], P(('cam', 'lmk')), may hold values from -1 to 3
- couplings: bfloat16 [10240, 576, 192], P(('cam', 'lmk')), may hold values from -0.09375 to 0.09375
- v_inverse: bfloat16 [1536, 192, 192], P('lmk'), may hold values from -3 to 4
- tile_cam: int32 [10240], P(('cam', 'lmk')), may hold values from 0 to 31
- tile_lmk: int32 [10240], P(('cam', 'lmk')), may hold values from 0 to 47
Outputs:
- solution: float32 [128, 32, 576], P(('cam', 'lmk'))
All inputs are finite; a program needn't handle non-finite values.
Results may differ from a plain program's by a relative error of at most 0.012.
Values may be sent and summed in bfloat16 or wider, within the bound.
A program may use at most 128 MiB of HBM per device.

v0:
```python
import jax
import jax.numpy as jnp
from jax import lax
from jax.sharding import PartitionSpec as P

POWERS = 4


def onehot_sum(selected, values):
    upper = values.astype(jnp.bfloat16)
    lower = (values - upper.astype(jnp.float32)).astype(jnp.bfloat16)
    first = jnp.einsum("st,tpx->spx", selected, upper, preferred_element_type=jnp.float32)
    second = jnp.einsum("st,tpx->spx", selected, lower, preferred_element_type=jnp.float32)
    return first + second


def local(probes, u_inverse, couplings, v_inverse, tile_cam, tile_lmk):
    group_size = lax.axis_size("lmk") * u_inverse.shape[0]
    landmark_count = v_inverse.shape[0]
    cam_onehot = (tile_cam[None, :] == jnp.arange(group_size, dtype=jnp.int32)[:, None]).astype(
        jnp.bfloat16
    )
    lmk_onehot = (tile_lmk[None, :] == jnp.arange(landmark_count, dtype=jnp.int32)[:, None]).astype(
        jnp.bfloat16
    )
    current = jnp.einsum("bpc,bcd->bpd", probes, u_inverse, preferred_element_type=jnp.float32)
    series_sum = current
    panel = lax.all_gather(current.astype(jnp.bfloat16), "lmk", axis=0, tiled=True)
    for power_step in range(POWERS):
        tile_rows = jnp.take(panel, tile_cam, axis=0)
        forward = jnp.einsum(
            "tpc,tcl->tpl", tile_rows, couplings, preferred_element_type=jnp.float32
        )
        partial_value = onehot_sum(lmk_onehot, forward)
        landmark_sum = lax.psum(partial_value, "cam")
        landmark_out = jnp.einsum(
            "mpl,mlq->mpq",
            landmark_sum.astype(jnp.bfloat16),
            v_inverse,
            preferred_element_type=jnp.float32,
        ).astype(jnp.bfloat16)
        picked = jnp.take(landmark_out, tile_lmk, axis=0)
        backward = jnp.einsum("tpl,tcl->tpc", picked, couplings, preferred_element_type=jnp.float32)
        camera_sum = lax.psum_scatter(
            onehot_sum(cam_onehot, backward), "lmk", scatter_dimension=0, tiled=True
        )
        current = jnp.einsum(
            "bpc,bcd->bpd",
            camera_sum.astype(jnp.bfloat16),
            u_inverse,
            preferred_element_type=jnp.float32,
        )
        series_sum = series_sum + current
        if power_step + 1 < POWERS:
            panel = lax.all_gather(current.astype(jnp.bfloat16), "lmk", axis=0, tiled=True)
    return series_sum


def solution(mesh):
    in_specs = (
        P(("cam", "lmk"), None, None),
        P(("cam", "lmk"), None, None),
        P(("cam", "lmk"), None, None),
        P("lmk", None, None),
        P(("cam", "lmk")),
        P(("cam", "lmk")),
    )
    out_specs = P(("cam", "lmk"), None, None)
    return jax.shard_map(local, mesh=mesh, in_specs=in_specs, out_specs=out_specs, check_vma=False)
```

profile of v0, /device:TPU:0, one launch (start us, length us, event | category | flops | bytes accessed | tf_op | source)
XLA Modules:
  0.0 1577.2 jit_solution(3444154400009519905)
XLA Ops:
  12.0 151.3 %all-gather.9.cloned.1.call-done = bf16[1024,576]{1,0:T(8,128)(2,1)} async-done(((bf16[32,576]{1,0:T(8,128)(2,1)}), bf16[1024,576]{1,0:T(8,128)(2,1)}) %all-gather.9.cloned.1.call-update) | async-done | bytes 1179664 | tf_op jit(solution)/shard_map/all_gather | solution.py:28
  163.3 4.2 gather_fusion
  167.5 11.5 subtract_convert_fusion.7
  181.1 34.3 %all-reduce.4 = bf16[48,32,192]{2,0,1:T(8,128)(2,1)} all-reduce(f32[48,32,192]{2,0,1:T(8,128)S(1)} %convolution_add_fusion.3), channel_id=1, replica_groups=mesh['cam'=4,'lmk'=32] {'cam'}, use_global_device_ids=true, to_apply=%region_0.0 | all-reduce | flops 294912 | bytes 1769472 | tf_op jit(solution)/shard_map/psum | solution.py:35
  215.4 3.3 convolution_convert_fusion.3
  219.4 11.3 subtract_convert_fusion.3
  233.7 3.0 copy.28
  236.8 166.0 %reduce-scatter.5.cloned.1.call-done = f32[1,32,576]{2,1,0:T(8,128)} async-done(((f32[32,32,576]{2,1,0:T(8,128)}), f32[1,32,576]{2,1,0:T(8,128)}) %reduce-scatter.5.cloned.1.call-update) | async-done | bytes 73744 | tf_op jit(solution)/shard_map/reduce_scatter | solution.py:44
  404.8 147.3 %all-gather.11.cloned.1.call-done = bf16[1024,576]{1,0:T(8,128)(2,1)} async-done(((bf16[32,576]{1,0:T(8,128)(2,1)}), bf16[1024,576]{1,0:T(8,128)(2,1)}) %all-gather.11.cloned.1.call-update) | async-done | bytes 1179664 | tf_op jit(solution)/shard_map/all_gather | solution.py:55
  552.0 4.2 gather_fusion.2
  556.2 11.5 subtract_convert_fusion.6
  569.8 34.1 %all-reduce.5 = bf16[48,32,192]{2,0,1:T(8,128)(2,1)} all-reduce(f32[48,32,192]{2,0,1:T(8,128)S(1)} %convolution_add_fusion.2), channel_id=1, replica_groups=mesh['cam'=4,'lmk'=32] {'cam'}, use_global_device_ids=true, to_apply=%region_2.0 | all-reduce | flops 294912 | bytes 1769472 | tf_op jit(solution)/shard_map/psum | solution.py:35
  603.9 3.3 convolution_convert_fusion.2
  607.9 11.3 subtract_convert_fusion.2
  622.1 3.0 copy.34
  625.2 166.1 %reduce-scatter.7.cloned.1.call-done = f32[1,32,576]{2,1,0:T(8,128)} async-done(((f32[32,32,576]{2,1,0:T(8,128)}), f32[1,32,576]{2,1,0:T(8,128)}) %reduce-scatter.7.cloned.1.call-update) | async-done | bytes 73744 | tf_op jit(solution)/shard_map/reduce_scatter | solution.py:44
  793.6 147.0 %all-gather.13.cloned.1.call-done = bf16[1024,576]{1,0:T(8,128)(2,1)} async-done(((bf16[32,576]{1,0:T(8,128)(2,1)}), bf16[1024,576]{1,0:T(8,128)(2,1)}) %all-gather.13.cloned.1.call-update) | async-done | bytes 1179664 | tf_op jit(solution)/shard_map/all_gather | solution.py:55
  940.7 4.2 gather_fusion.4
  944.9 11.5 subtract_convert_fusion.5
  958.4 34.1 %all-reduce.6 = bf16[48,32,192]{2,0,1:T(8,128)(2,1)} all-reduce(f32[48,32,192]{2,0,1:T(8,128)S(1)} %convolution_add_fusion.1), channel_id=1, replica_groups=mesh['cam'=4,'lmk'=32] {'cam'}, use_global_device_ids=true, to_apply=%region_4.7 | all-reduce | flops 294912 | bytes 1769472 | tf_op jit(solution)/shard_map/psum | solution.py:35
  992.5 3.3 convolution_convert_fusion.1
  996.5 11.3 subtract_convert_fusion.1
  1010.8 3.0 copy.40
  1013.9 165.9 %reduce-scatter.9.cloned.1.call-done = f32[1,32,576]{2,1,0:T(8,128)} async-done(((f32[32,32,576]{2,1,0:T(8,128)}), f32[1,32,576]{2,1,0:T(8,128)}) %reduce-scatter.9.cloned.1.call-update) | async-done | bytes 73744 | tf_op jit(solution)/shard_map/reduce_scatter | solution.py:44
  1181.7 147.5 %all-gather.15.cloned.1.call-done = bf16[1024,576]{1,0:T(8,128)(2,1)} async-done(((bf16[32,576]{1,0:T(8,128)(2,1)}), bf16[1024,576]{1,0:T(8,128)(2,1)}) %all-gather.15.cloned.1.call-update) | async-done | bytes 1179664 | tf_op jit(solution)/shard_map/all_gather | solution.py:55
  1329.2 4.2 gather_fusion.6
  1333.4 11.5 subtract_convert_fusion.4
  1347.0 34.1 %all-reduce.7 = bf16[48,32,192]{2,0,1:T(8,128)(2,1)} all-reduce(f32[48,32,192]{2,0,1:T(8,128)S(1)} %convolution_add_fusion), channel_id=1, replica_groups=mesh['cam'=4,'lmk'=32] {'cam'}, use_global_device_ids=true, to_apply=%region_6.9 | all-reduce | flops 294912 | bytes 1769472 | tf_op jit(solution)/shard_map/psum | solution.py:35
  1381.0 3.3 convolution_convert_fusion
  1385.1 11.3 subtract_convert_fusion
  1399.3 3.0 copy.46
  1402.4 166.1 %reduce-scatter.11.cloned.1.call-done = f32[1,32,576]{2,1,0:T(8,128)} async-done(((f32[32,32,576]{2,1,0:T(8,128)}), f32[1,32,576]{2,1,0:T(8,128)}) %reduce-scatter.11.cloned.1.call-update) | async-done | bytes 73744 | tf_op jit(solution)/shard_map/reduce_scatter | solution.py:44
  (55 shorter events, 36.4 us)
Async XLA Ops:
  6.5 1.1 copy-start
  6.5 156.8 %all-gather.9.cloned.1.call-start = ((), (), s32[]{:S(2)}) async-start(), calls=%async_computation.8 | async-start | bytes 1351680 | tf_op jit(solution)/shard_map/all_gather | solution.py:28
  9.3 393.4 %reduce-scatter.5.cloned.1.call-start = ((), (), s32[]{:S(2)}) async-start(), calls=%async_computation.4 | async-start | bytes 2703360 | tf_op jit(solution)/shard_map/reduce_scatter | solution.py:44
  167.5 11.5 copy-start.2
  219.4 11.3 copy-start.3
  236.7 315.3 %all-gather.11.cloned.1.call-start = ((), (), s32[]{:S(2)}) async-start(), calls=%async_computation.9 | async-start | bytes 1351680 | tf_op jit(solution)/shard_map/all_gather | solution.py:55
  404.5 386.9 %reduce-scatter.7.cloned.1.call-start = ((), (), s32[]{:S(2)}) async-start(), calls=%async_computation.5 | async-start | bytes 2703360 | tf_op jit(solution)/shard_map/reduce_scatter | solution.py:44
  625.2 315.5 %all-gather.13.cloned.1.call-start = ((), (), s32[]{:S(2)}) async-start(), calls=%async_computation.10 | async-start | bytes 1351680 | tf_op jit(solution)/shard_map/all_gather | solution.py:55
  793.1 386.6 %reduce-scatter.9.cloned.1.call-start = ((), (), s32[]{:S(2)}) async-start(), calls=%async_computation.6 | async-start | bytes 2703360 | tf_op jit(solution)/shard_map/reduce_scatter | solution.py:44
  1013.8 315.4 %all-gather.15.cloned.1.call-start = ((), (), s32[]{:S(2)}) async-start(), calls=%async_computation.11 | async-start | bytes 1351680 | tf_op jit(solution)/shard_map/all_gather | solution.py:55
  1181.5 386.9 %reduce-scatter.11.cloned.1.call-start = ((), (), s32[]{:S(2)}) async-start(), calls=%async_computation.7 | async-start | bytes 2703360 | tf_op jit(solution)/shard_map/reduce_scatter | solution.py:44
  1402.3 166.1 %copy-start.1 = (f32[32,576]{1,0:T(8,128)S(1)}, f32[32,576]{1,0:T(8,128)}, u32[]{:S(2)}) copy-start(f32[32,576]{1,0:T(8,128)} %get-tuple-element.24) | copy-start | bytes 221188
Sparse Core Ops, SparseCore 0:
  9.5 153.8 all-gather.8
  236.8 165.8 reduce-scatter.4
  404.6 147.3 all-gather.10
  625.3 166.0 reduce-scatter.6
  793.2 147.3 all-gather.12
  1014.0 165.7 reduce-scatter.8
  1181.6 147.5 all-gather.14
  1402.5 165.9 reduce-scatter.10
where the time goes:
time: 1580 us
  waiting for transfers between devices  1260 us (80%)
  blocking collectives  136 us (9%)
  matrix products  133 us (8%)
  local copies, waits for them, and re-layouts  32.7 us (2%)
    reduce_scatter x4, waiting for transfers between devices, local(): lax.psum_scatter(onehot_sum(cam_onehot, backward), 'lmk', scatter_dimensi...  664 us
    all_gather x4, waiting for transfers between devices, local(): lax.all_gather(current.astype(jnp.bfloat16), 'lmk', axis=0, tiled=True)  593 us
    psum x4, blocking collectives, local(): landmark_sum = lax.psum(partial_value, 'cam')  136 us
    dot_general x4, matrix products, local(): jnp.einsum('tpc,tcl->tpl', tile_rows, couplings, preferred_element_type=j...  46.1 us
    dot_general x4, matrix products, local(): jnp.einsum('tpl,tcl->tpc', picked, couplings, preferred_element_type=jnp....  45 us
  transfers between devices with their start and end apart: 8, of which 8 were waited for; matrix products, arithmetic and copies ran while one was open for 0% of the time, Pallas kernels for 0%

commit v1 on v0

--- a/solution.py
+++ b/solution.py
@@ -14,6 +14,27 @@
     return first + second
 
 
+def a2a_gather(block, axis_name):
+    size = lax.axis_size(axis_name)
+    tiled = jnp.broadcast_to(block[None], (size,) + block.shape)
+    got = lax.all_to_all(tiled, axis_name, 0, 0, tiled=False)
+    return got.reshape((size * block.shape[0],) + block.shape[1:])
+
+
+def a2a_reduce_scatter(full, axis_name):
+    size = lax.axis_size(axis_name)
+    chunks = full.reshape((size, full.shape[0] // size) + full.shape[1:])
+    got = lax.all_to_all(chunks, axis_name, 0, 0, tiled=False)
+    return jnp.sum(got, axis=0)
+
+
+def a2a_allreduce(full, axis_name):
+    size = lax.axis_size(axis_name)
+    tiled = jnp.broadcast_to(full[None], (size,) + full.shape)
+    got = lax.all_to_all(tiled, axis_name, 0, 0, tiled=False)
+    return jnp.sum(got, axis=0)
+
+
 def local(probes, u_inverse, couplings, v_inverse, tile_cam, tile_lmk):
     group_size = lax.axis_size("lmk") * u_inverse.shape[0]
     landmark_count = v_inverse.shape[0]
@@ -25,14 +46,14 @@
     )
     current = jnp.einsum("bpc,bcd->bpd", probes, u_inverse, preferred_element_type=jnp.float32)
     series_sum = current
-    panel = lax.all_gather(current.astype(jnp.bfloat16), "lmk", axis=0, tiled=True)
+    panel = a2a_gather(current.astype(jnp.bfloat16), "lmk")
     for power_step in range(POWERS):
         tile_rows = jnp.take(panel, tile_cam, axis=0)
         forward = jnp.einsum(
             "tpc,tcl->tpl", tile_rows, couplings, preferred_element_type=jnp.float32
         )
         partial_value = onehot_sum(lmk_onehot, forward)
-        landmark_sum = lax.psum(partial_value, "cam")
+        landmark_sum = a2a_allreduce(partial_value, "cam")
         landmark_out = jnp.einsum(
             "mpl,mlq->mpq",
             landmark_sum.astype(jnp.bfloat16),
@@ -41,9 +62,7 @@
         ).astype(jnp.bfloat16)
         picked = jnp.take(landmark_out, tile_lmk, axis=0)
         backward = jnp.einsum("tpl,tcl->tpc", picked, couplings, preferred_element_type=jnp.float32)
-        camera_sum = lax.psum_scatter(
-            onehot_sum(cam_onehot, backward), "lmk", scatter_dimension=0, tiled=True
-        )
+        camera_sum = a2a_reduce_scatter(onehot_sum(cam_onehot, backward), "lmk")
         current = jnp.einsum(
             "bpc,bcd->bpd",
             camera_sum.astype(jnp.bfloat16),
@@ -52,7 +71,7 @@
         )
         series_sum = series_sum + current
         if power_step + 1 < POWERS:
-            panel = lax.all_gather(current.astype(jnp.bfloat16), "lmk", axis=0, tiled=True)
+            panel = a2a_gather(current.astype(jnp.bfloat16), "lmk")
     return series_sum
 
 

time: 1580 us -> 741 us (0.47)
  waiting for transfers between devices: 1260 us -> 91.3 us
  blocking collectives: 136 us -> 447 us
    reduce_scatter x4 -> x0, waiting for transfers between devices: 664 us -> none  [local(): lax.psum_scatter(onehot_sum(cam_onehot, backward), 'lmk', scatter_dimensi...]
    all_gather x4 -> x0, waiting for transfers between devices: 593 us -> none  [local(): lax.all_gather(current.astype(jnp.bfloat16), 'lmk', axis=0, tiled=True)]
    all_to_all x0 -> x10, blocking collectives: none -> 447 us  [the longest x3 228 us: a2a_allreduce(): got = lax.all_to_all(tiled, axis_name, 0, 0, tiled=False)]
    psum x4 -> x0, blocking collectives: 136 us -> none  [local(): landmark_sum = lax.psum(partial_value, 'cam')]
    all_to_all x0 -> x2, waiting for transfers between devices: none -> 91.3 us  [the longest x1 72.1 us: a2a_allreduce(): got = lax.all_to_all(tiled, axis_name, 0, 0, tiled=False)]
    reduce_sum x0 -> x8, other arithmetic: none -> 17.2 us  [the longest x4 16.1 us: a2a_allreduce(): return jnp.sum(got, axis=0)]
  transfers between devices with their start and end apart: 8 -> 2, of which waited for: 8 -> 2; matrix products, arithmetic and copies ran while one was open for 0% -> 0% of each run, Pallas kernels for 0% -> 0%
where the time goes in v1:
time: 741 us; the launch traced here: 734 us
  blocking collectives  447 us (60%)
  matrix products  131 us (18%)
  waiting for transfers between devices  91.3 us (12%)
  local copies, waits for them, and re-layouts  32.7 us (4%)
  other arithmetic  17.3 us (2%)
  starting transfers between devices  14.2 us (2%)
    all_to_all x3, blocking collectives, a2a_allreduce(): got = lax.all_to_all(tiled, axis_name, 0, 0, tiled=False)  228 us
    all_to_all x4, blocking collectives, a2a_reduce_scatter(): got = lax.all_to_all(chunks, axis_name, 0, 0, tiled=False)  151 us
    all_to_all x1, waiting for transfers between devices, a2a_allreduce(): got = lax.all_to_all(tiled, axis_name, 0, 0, tiled=False)  72.1 us
    all_to_all x3, blocking collectives, a2a_gather(): got = lax.all_to_all(tiled, axis_name, 0, 0, tiled=False)  68.8 us
    dot_general x4, matrix products, local(): jnp.einsum('tpc,tcl->tpl', tile_rows, couplings, preferred_element_type=j...  46.2 us
    dot_general x4, matrix products, local(): jnp.einsum('tpl,tcl->tpc', picked, couplings, preferred_element_type=jnp....  45 us
    all_to_all x1, waiting for transfers between devices, a2a_gather(): got = lax.all_to_all(tiled, axis_name, 0, 0, tiled=False)  19.2 us
    reduce_sum x4, other arithmetic, a2a_allreduce(): return jnp.sum(got, axis=0)  16.1 us
  transfers between devices with their start and end apart: 2, of which 2 were waited for; matrix products, arithmetic and copies ran while one was open for 0% of the time, Pallas kernels for 0%

profile of v1, /device:TPU:0, one launch (start us, length us, event | category | flops | bytes accessed | tf_op | source)
XLA Modules:
  0.0 734.4 jit_solution(9106531578861382186)
XLA Ops:
  3.9 8.8 %all-to-all-start = ((bf16[32,1,32,576]{3,2,1,0:T(8,128)(2,1)}), bf16[32,1,32,576]{3,2,1,0:T(8,128)(2,1)S(1)}, u32[]{:S(2)}, u32[]{:S(2)}) async-start(bf16[32,1,32,576]{3,2,1,0:T(8,128)(2,1)} %broadcast_in_dim.34), calls=%async_computation | async-start | bytes 2621440 | tf_op jit(solution)/shard_map/all_to_all | solution.py:20
  12.8 19.2 %all-to-all-done = bf16[32,1,32,576]{3,2,1,0:T(8,128)(2,1)S(1)} async-done(((bf16[32,1,32,576]{3,2,1,0:T(8,128)(2,1)}), bf16[32,1,32,576]{3,2,1,0:T(8,128)(2,1)S(1)}, u32[]{:S(2)}, u32[]{:S(2)}) %all-to-all-start) | async-done | bytes 1179680 | tf_op jit(solution)/shard_map/all_to_all | solution.py:20
  32.0 2.9 gather_fusion
  34.9 11.5 %subtract_convert_fusion.7 = (bf16[80,32,192]{2,1,0:T(8,128)(2,1)S(1)}, bf16[80,32,192]{2,1,0:T(8,128)(2,1)S(1)}) fusion(bf16[80,576,192]{1,2,0:T(8,128)(2,1)} %param.12, bf16[80,32,576]{2,1,0:T(8,128)(2,1)} %gather_fusion, pred[80]{0:T(512)(128)(4,1)S(1)} %compare_and_fusion.1), kind=kOutput, calls=%fused_computation.47 | convolution fusion | flops 569671680 | bytes 22610000 | tf_op jit(solution)/shard_map/tpc,tcl->tpl/dot_general | solution.py:52
  49.4 3.5 broadcast_in_dim.35
  52.9 5.5 all-to-all-start.1
  58.4 72.1 %all-to-all-done.1 = f32[4,48,32,192]{3,2,1,0:T(8,128)} async-done(((f32[4,48,32,192]{3,2,1,0:T(8,128)}), f32[4,48,32,192]{3,2,1,0:T(8,128)}, u32[]{:S(2)}, u32[]{:S(2)}) %all-to-all-start.1) | async-done | bytes 4718624 | tf_op jit(solution)/shard_map/all_to_all | solution.py:34
  130.5 4.0 reduce_sum.72
  134.5 3.3 convolution_convert_fusion.3
  138.5 11.3 %subtract_convert_fusion.3 = (bf16[80,32,576]{2,1,0:T(8,128)(2,1)S(1)}, bf16[80,32,576]{2,1,0:T(8,128)(2,1)S(1)}) fusion(bf16[80,576,192]{1,2,0:T(8,128)(2,1)} %param.12, bf16[80,32,192]{2,1,0:T(8,128)(2,1)S(1)} %gather_fusion.1, pred[80]{0:T(512)(128)(4,1)S(1)} %compare_and_fusion), kind=kOutput, calls=%fused_computation.11 | convolution fusion | flops 572620800 | bytes 24576080 | tf_op jit(solution)/shard_map/tpl,tcl->tpc/dot_general | solution.py:64
  154.3 38.5 %all_to_all.60 = f32[32,1,32,576]{3,2,1,0:T(8,128)S(1)} all-to-all(f32[32,1,32,576]{3,2,1,0:T(8,128)S(1)} %copy.32), channel_id=1, replica_groups=mesh['cam'=4,'lmk'=32] {'lmk'}, dimensions={0} | all-to-all | bytes 4718592 | tf_op jit(solution)/shard_map/all_to_all | solution.py:27
  193.9 23.0 %all_to_all.61 = bf16[32,1,32,576]{3,2,1,0:T(8,128)(2,1)S(1)} all-to-all(bf16[32,1,32,576]{3,2,1,0:T(8,128)(2,1)S(1)} %broadcast_in_dim.36), channel_id=1, replica_groups=mesh['cam'=4,'lmk'=32] {'lmk'}, dimensions={0} | all-to-all | bytes 2359296 | tf_op jit(solution)/shard_map/all_to_all | solution.py:20
  219.8 11.5 %subtract_convert_fusion.6 = (bf16[80,32,192]{2,1,0:T(8,128)(2,1)S(1)}, bf16[80,32,192]{2,1,0:T(8,128)(2,1)S(1)}) fusion(bf16[80,576,192]{1,2,0:T(8,128)(2,1)} %param.12, bf16[80,32,576]{2,1,0:T(8,128)(2,1)} %gather_fusion.2, pred[80]{0:T(512)(128)(4,1)S(1)} %compare_and_fusion.1), kind=kOutput, calls=%fused_computation.45 | convolution fusion | flops 569671680 | bytes 22610000 | tf_op jit(solution)/shard_map/tpc,tcl->tpl/dot_general | solution.py:52
  235.1 76.2 %all_to_all.62 = f32[4,48,32,192]{3,2,1,0:T(8,128)} all-to-all(f32[4,48,32,192]{3,2,1,0:T(8,128)S(1)} %broadcast_in_dim.37), channel_id=1, replica_groups=mesh['cam'=4,'lmk'=32] {'cam'}, dimensions={0} | all-to-all | bytes 9437184 | tf_op jit(solution)/shard_map/all_to_all | solution.py:34
  311.3 4.0 reduce_sum.74
  315.3 3.3 convolution_convert_fusion.2
  319.3 11.3 %subtract_convert_fusion.2 = (bf16[80,32,576]{2,1,0:T(8,128)(2,1)S(1)}, bf16[80,32,576]{2,1,0:T(8,128)(2,1)S(1)}) fusion(bf16[80,576,192]{1,2,0:T(8,128)(2,1)} %param.12, bf16[80,32,192]{2,1,0:T(8,128)(2,1)S(1)} %gather_fusion.3, pred[80]{0:T(512)(128)(4,1)S(1)} %compare_and_fusion), kind=kOutput, calls=%fused_computation.10 | convolution fusion | flops 572620800 | bytes 24576080 | tf_op jit(solution)/shard_map/tpl,tcl->tpc/dot_general | solution.py:64
  335.1 37.3 %all_to_all.63 = f32[32,1,32,576]{3,2,1,0:T(8,128)S(1)} all-to-all(f32[32,1,32,576]{3,2,1,0:T(8,128)S(1)} %copy.38), channel_id=1, replica_groups=mesh['cam'=4,'lmk'=32] {'lmk'}, dimensions={0} | all-to-all | bytes 4718592 | tf_op jit(solution)/shard_map/all_to_all | solution.py:27
  373.6 22.9 %all_to_all.64 = bf16[32,1,32,576]{3,2,1,0:T(8,128)(2,1)S(1)} all-to-all(bf16[32,1,32,576]{3,2,1,0:T(8,128)(2,1)S(1)} %broadcast_in_dim.38), channel_id=1, replica_groups=mesh['cam'=4,'lmk'=32] {'lmk'}, dimensions={0} | all-to-all | bytes 2359296 | tf_op jit(solution)/shard_map/all_to_all | solution.py:20
  399.4 11.5 %subtract_convert_fusion.5 = (bf16[80,32,192]{2,1,0:T(8,128)(2,1)S(1)}, bf16[80,32,192]{2,1,0:T(8,128)(2,1)S(1)}) fusion(bf16[80,576,192]{1,2,0:T(8,128)(2,1)} %param.12, bf16[80,32,576]{2,1,0:T(8,128)(2,1)} %gather_fusion.4, pred[80]{0:T(512)(128)(4,1)S(1)} %compare_and_fusion.1), kind=kOutput, calls=%fused_computation.43 | convolution fusion | flops 569671680 | bytes 22610000 | tf_op jit(solution)/shard_map/tpc,tcl->tpl/dot_general | solution.py:52
  414.7 75.9 %all_to_all.65 = f32[4,48,32,192]{3,2,1,0:T(8,128)} all-to-all(f32[4,48,32,192]{3,2,1,0:T(8,128)S(1)} %broadcast_in_dim.39), channel_id=1, replica_groups=mesh['cam'=4,'lmk'=32] {'cam'}, dimensions={0} | all-to-all | bytes 9437184 | tf_op jit(solution)/shard_map/all_to_all | solution.py:34
  490.6 4.0 reduce_sum.76
  494.6 3.3 convolution_convert_fusion.1
  498.6 11.3 %subtract_convert_fusion.1 = (bf16[80,32,576]{2,1,0:T(8,128)(2,1)S(1)}, bf16[80,32,576]{2,1,0:T(8,128)(2,1)S(1)}) fusion(bf16[80,576,192]{1,2,0:T(8,128)(2,1)} %param.12, bf16[80,32,192]{2,1,0:T(8,128)(2,1)S(1)} %gather_fusion.5, pred[80]{0:T(512)(128)(4,1)S(1)} %compare_and_fusion), kind=kOutput, calls=%fused_computation.9 | convolution fusion | flops 572620800 | bytes 24576080 | tf_op jit(solution)/shard_map/tpl,tcl->tpc/dot_general | solution.py:64
  514.4 37.3 %all_to_all.66 = f32[32,1,32,576]{3,2,1,0:T(8,128)S(1)} all-to-all(f32[32,1,32,576]{3,2,1,0:T(8,128)S(1)} %copy.44), channel_id=1, replica_groups=mesh['cam'=4,'lmk'=32] {'lmk'}, dimensions={0} | all-to-all | bytes 4718592 | tf_op jit(solution)/shard_map/all_to_all | solution.py:27
  552.9 23.0 %all_to_all.67 = bf16[32,1,32,576]{3,2,1,0:T(8,128)(2,1)S(1)} all-to-all(bf16[32,1,32,576]{3,2,1,0:T(8,128)(2,1)S(1)} %broadcast_in_dim.40), channel_id=1, replica_groups=mesh['cam'=4,'lmk'=32] {'lmk'}, dimensions={0} | all-to-all | bytes 2359296 | tf_op jit(solution)/shard_map/all_to_all | solution.py:20
  578.7 11.5 %subtract_convert_fusion.4 = (bf16[80,32,192]{2,1,0:T(8,128)(2,1)S(1)}, bf16[80,32,192]{2,1,0:T(8,128)(2,1)S(1)}) fusion(bf16[80,576,192]{1,2,0:T(8,128)(2,1)} %param.12, bf16[80,32,576]{2,1,0:T(8,128)(2,1)} %gather_fusion.6, pred[80]{0:T(512)(128)(4,1)S(1)} %compare_and_fusion.1), kind=kOutput, calls=%fused_computation.41 | convolution fusion | flops 569671680 | bytes 22610000 | tf_op jit(solution)/shard_map/tpc,tcl->tpl/dot_general | solution.py:52
  594.0 76.0 %all_to_all.68 = f32[4,48,32,192]{3,2,1,0:T(8,128)} all-to-all(f32[4,48,32,192]{3,2,1,0:T(8,128)S(1)} %broadcast_in_dim.41), channel_id=1, replica_groups=mesh['cam'=4,'lmk'=32] {'cam'}, dimensions={0} | all-to-all | bytes 9437184 | tf_op jit(solution)/shard_map/all_to_all | solution.py:34
  670.0 4.0 reduce_sum.78
  674.0 3.3 convolution_convert_fusion
  678.1 11.3 %subtract_convert_fusion = (bf16[80,32,576]{2,1,0:T(8,128)(2,1)S(1)}, bf16[80,32,576]{2,1,0:T(8,128)(2,1)S(1)}) fusion(bf16[80,576,192]{1,2,0:T(8,128)(2,1)} %param.12, bf16[80,32,192]{2,1,0:T(8,128)(2,1)S(1)} %gather_fusion.7, pred[80]{0:T(512)(128)(4,1)S(1)} %compare_and_fusion), kind=kOutput, calls=%fused_computation.8 | convolution fusion | flops 572620800 | bytes 24576080 | tf_op jit(solution)/shard_map/tpl,tcl->tpc/dot_general | solution.py:64
  693.8 37.3 %all_to_all.69 = f32[32,1,32,576]{3,2,1,0:T(8,128)S(1)} all-to-all(f32[32,1,32,576]{3,2,1,0:T(8,128)S(1)} %copy.50), channel_id=1, replica_groups=mesh['cam'=4,'lmk'=32] {'lmk'}, dimensions={0} | all-to-all | bytes 4718592 | tf_op jit(solution)/shard_map/all_to_all | solution.py:27
  (63 shorter events, 53.7 us)
Async XLA Ops:
  0.0 1.1 copy-start
  0.0 12.7 %copy-start.4 = (s32[80]{0:T(128)S(1)}, s32[80]{0:T(128)}, u32[]{:S(2)}) copy-start(s32[80]{0:T(128)} %param.14) | copy-start | bytes 964
  3.9 28.0 %all-to-all-start = ((bf16[32,1,32,576]{3,2,1,0:T(8,128)(2,1)}), bf16[32,1,32,576]{3,2,1,0:T(8,128)(2,1)S(1)}, u32[]{:S(2)}, u32[]{:S(2)}) async-start(bf16[32,1,32,576]{3,2,1,0:T(8,128)(2,1)} %broadcast_in_dim.34), calls=%async_computation | async-start | bytes 2621440 | tf_op jit(solution)/shard_map/all_to_all | solution.py:20
  34.9 11.6 %copy-start.3 = (s32[80]{0:T(128)S(1)}, s32[80]{0:T(128)}, u32[]{:S(2)}) copy-start(s32[80]{0:T(128)} %param.15) | copy-start | bytes 964
  52.9 77.6 %all-to-all-start.1 = ((f32[4,48,32,192]{3,2,1,0:T(8,128)}), f32[4,48,32,192]{3,2,1,0:T(8,128)}, u32[]{:S(2)}, u32[]{:S(2)}) async-start(f32[4,48,32,192]{3,2,1,0:T(8,128)} %broadcast_in_dim.35), calls=%async_computation.1 | async-start | bytes 12582912 | tf_op jit(solution)/shard_map/all_to_all | solution.py:34
  731.2 0.9 copy-start.1
  731.2 0.9 copy-start.2

commit v2 on v1

--- a/solution.py
+++ b/solution.py
@@ -44,6 +44,9 @@
     lmk_onehot = (tile_lmk[None, :] == jnp.arange(landmark_count, dtype=jnp.int32)[:, None]).astype(
         jnp.bfloat16
     )
+    cam_count = lax.axis_size("cam")
+    part_size = landmark_count // cam_count
+    v_part = lax.dynamic_slice_in_dim(v_inverse, lax.axis_index("cam") * part_size, part_size, 0)
     current = jnp.einsum("bpc,bcd->bpd", probes, u_inverse, preferred_element_type=jnp.float32)
     series_sum = current
     panel = a2a_gather(current.astype(jnp.bfloat16), "lmk")
@@ -53,13 +56,14 @@
             "tpc,tcl->tpl", tile_rows, couplings, preferred_element_type=jnp.float32
         )
         partial_value = onehot_sum(lmk_onehot, forward)
-        landmark_sum = a2a_allreduce(partial_value, "cam")
-        landmark_out = jnp.einsum(
+        landmark_part = a2a_reduce_scatter(partial_value, "cam")
+        landmark_part_out = jnp.einsum(
             "mpl,mlq->mpq",
-            landmark_sum.astype(jnp.bfloat16),
-            v_inverse,
+            landmark_part.astype(jnp.bfloat16),
+            v_part,
             preferred_element_type=jnp.float32,
         ).astype(jnp.bfloat16)
+        landmark_out = a2a_gather(landmark_part_out, "cam")
         picked = jnp.take(landmark_out, tile_lmk, axis=0)
         backward = jnp.einsum("tpl,tcl->tpc", picked, couplings, preferred_element_type=jnp.float32)
         camera_sum = a2a_reduce_scatter(onehot_sum(cam_onehot, backward), "lmk")

time: 741 us -> 571 us (0.77)
  blocking collectives: 447 us -> 339 us
  waiting for transfers between devices: 91.3 us -> 53.8 us
  other arithmetic: 17.3 us -> 1.79 us
  matrix products: 131 us -> 123 us
    all_to_all x3 -> x0, blocking collectives: 228 us -> none  [a2a_allreduce(): got = lax.all_to_all(tiled, axis_name, 0, 0, tiled=False)]
    all_to_all x4 -> x7, blocking collectives: 151 us -> 223 us  [a2a_reduce_scatter(): got = lax.all_to_all(chunks, axis_name, 0, 0, tiled=False)]
    all_to_all x1, waiting for transfers between devices: 72.1 us -> 21.6 us  [a2a_reduce_scatter(): got = lax.all_to_all(chunks, axis_name, 0, 0, tiled=False)]
    all_to_all x3 -> x6, blocking collectives: 68.8 us -> 116 us  [a2a_gather(): got = lax.all_to_all(tiled, axis_name, 0, 0, tiled=False)]
    reduce_sum x4 -> x0, other arithmetic: 16.1 us -> none  [a2a_allreduce(): return jnp.sum(got, axis=0)]
    all_to_all x1 -> x2, waiting for transfers between devices: 19.2 us -> 32.2 us  [a2a_gather(): got = lax.all_to_all(tiled, axis_name, 0, 0, tiled=False)]
  transfers between devices with their start and end apart: 2 -> 3, of which waited for: 2 -> 3; matrix products, arithmetic and copies ran while one was open for 0% -> 0% of each run, Pallas kernels for 0% -> 0%
where the time goes in v2:
time: 571 us; the launch traced here: 565 us
  blocking collectives  339 us (59%)
  matrix products  123 us (22%)
  waiting for transfers between devices  53.8 us (9%)
  local copies, waits for them, and re-layouts  29.2 us (5%)
  starting transfers between devices  17.3 us (3%)
    all_to_all x7, blocking collectives, a2a_reduce_scatter(): got = lax.all_to_all(chunks, axis_name, 0, 0, tiled=False)  223 us
    all_to_all x6, blocking collectives, a2a_gather(): got = lax.all_to_all(tiled, axis_name, 0, 0, tiled=False)  116 us
    dot_general x4, matrix products, local(): jnp.einsum('tpc,tcl->tpl', tile_rows, couplings, preferred_element_type=j...  46.1 us
    dot_general x4, matrix products, local(): jnp.einsum('tpl,tcl->tpc', picked, couplings, preferred_element_type=jnp....  45 us
    all_to_all x2, waiting for transfers between devices, a2a_gather(): got = lax.all_to_all(tiled, axis_name, 0, 0, tiled=False)  32.2 us
    all_to_all x1, waiting for transfers between devices, a2a_reduce_scatter(): got = lax.all_to_all(chunks, axis_name, 0, 0, tiled=False)  21.6 us
    all_to_all x2, starting transfers between devices, a2a_gather(): got = lax.all_to_all(tiled, axis_name, 0, 0, tiled=False)  12.4 us
    gather x4, local copies, waits for them, and re-layouts, local(): tile_rows = jnp.take(panel, tile_cam, axis=0)  11.6 us
  transfers between devices with their start and end apart: 3, of which 3 were waited for; matrix products, arithmetic and copies ran while one was open for 0% of the time, Pallas kernels for 0%

profile of v2, /device:TPU:0, one launch (start us, length us, event | category | flops | bytes accessed | tf_op | source)
XLA Modules:
  0.0 564.7 jit_solution(10759579085218902589)
XLA Ops:
  3.9 8.8 %all-to-all-start = ((bf16[32,1,32,576]{3,2,1,0:T(8,128)(2,1)}), bf16[32,1,32,576]{3,2,1,0:T(8,128)(2,1)S(1)}, u32[]{:S(2)}, u32[]{:S(2)}) async-start(bf16[32,1,32,576]{3,2,1,0:T(8,128)(2,1)} %broadcast_in_dim.34), calls=%async_computation | async-start | bytes 2621440 | tf_op jit(solution)/shard_map/all_to_all | solution.py:20
  12.8 19.2 %all-to-all-done = bf16[32,1,32,576]{3,2,1,0:T(8,128)(2,1)S(1)} async-done(((bf16[32,1,32,576]{3,2,1,0:T(8,128)(2,1)}), bf16[32,1,32,576]{3,2,1,0:T(8,128)(2,1)S(1)}, u32[]{:S(2)}, u32[]{:S(2)}) %all-to-all-start) | async-done | bytes 1179680 | tf_op jit(solution)/shard_map/all_to_all | solution.py:20
  32.0 2.9 gather_fusion
  34.9 11.5 %subtract_convert_fusion.7 = (bf16[80,32,192]{2,1,0:T(8,128)(2,1)S(1)}, bf16[80,32,192]{2,1,0:T(8,128)(2,1)S(1)}) fusion(bf16[80,576,192]{1,2,0:T(8,128)(2,1)} %param.12, bf16[80,32,576]{2,1,0:T(8,128)(2,1)} %gather_fusion, pred[80]{0:T(512)(128)(4,1)S(1)} %compare_and_fusion.1), kind=kOutput, calls=%fused_computation.47 | convolution fusion | flops 569671680 | bytes 22610000 | tf_op jit(solution)/shard_map/tpc,tcl->tpl/dot_general | solution.py:55
  48.4 2.1 copy.45
  50.5 4.9 all-to-all-start.1
  55.4 21.6 %all-to-all-done.1 = f32[4,12,32,192]{3,2,1,0:T(8,128)S(1)} async-done(((f32[4,12,32,192]{3,2,1,0:T(8,128)}), f32[4,12,32,192]{3,2,1,0:T(8,128)S(1)}, u32[]{:S(2)}, u32[]{:S(2)}) %all-to-all-start.1) | async-done | bytes 1179680 | tf_op jit(solution)/shard_map/all_to_all | solution.py:27
  79.6 3.7 all-to-all-start.2
  83.4 13.0 %all-to-all-done.2 = bf16[4,12,32,192]{3,2,1,0:T(8,128)(2,1)S(1)} async-done(((bf16[4,12,32,192]{3,2,1,0:T(8,128)(2,1)}), bf16[4,12,32,192]{3,2,1,0:T(8,128)(2,1)S(1)}, u32[]{:S(2)}, u32[]{:S(2)}) %all-to-all-start.2) | async-done | bytes 589856 | tf_op jit(solution)/shard_map/all_to_all | solution.py:20
  97.1 11.3 %subtract_convert_fusion.3 = (bf16[80,32,576]{2,1,0:T(8,128)(2,1)S(1)}, bf16[80,32,576]{2,1,0:T(8,128)(2,1)S(1)}) fusion(bf16[80,576,192]{1,2,0:T(8,128)(2,1)} %param.12, bf16[80,32,192]{2,1,0:T(8,128)(2,1)S(1)} %gather_fusion.1, pred[80]{0:T(512)(128)(4,1)S(1)} %compare_and_fusion), kind=kOutput, calls=%fused_computation.11 | convolution fusion | flops 572620800 | bytes 24576080 | tf_op jit(solution)/shard_map/tpl,tcl->tpc/dot_general | solution.py:68
  112.8 38.5 %all_to_all.80 = f32[32,1,32,576]{3,2,1,0:T(8,128)S(1)} all-to-all(f32[32,1,32,576]{3,2,1,0:T(8,128)S(1)} %copy.48), channel_id=1, replica_groups=mesh['cam'=4,'lmk'=32] {'lmk'}, dimensions={0} | all-to-all | bytes 4718592 | tf_op jit(solution)/shard_map/all_to_all | solution.py:27
  151.8 23.0 %all_to_all.81 = bf16[32,1,32,576]{3,2,1,0:T(8,128)(2,1)S(1)} all-to-all(bf16[32,1,32,576]{3,2,1,0:T(8,128)(2,1)S(1)} %broadcast_in_dim.36), channel_id=1, replica_groups=mesh['cam'=4,'lmk'=32] {'lmk'}, dimensions={0} | all-to-all | bytes 2359296 | tf_op jit(solution)/shard_map/all_to_all | solution.py:20
  174.8 2.9 gather_fusion.2
  177.7 11.5 %subtract_convert_fusion.6 = (bf16[80,32,192]{2,1,0:T(8,128)(2,1)S(1)}, bf16[80,32,192]{2,1,0:T(8,128)(2,1)S(1)}) fusion(bf16[80,576,192]{1,2,0:T(8,128)(2,1)} %param.12, bf16[80,32,576]{2,1,0:T(8,128)(2,1)} %gather_fusion.2, pred[80]{0:T(512)(128)(4,1)S(1)} %compare_and_fusion.1), kind=kOutput, calls=%fused_computation.45 | convolution fusion | flops 569671680 | bytes 22610000 | tf_op jit(solution)/shard_map/tpc,tcl->tpl/dot_general | solution.py:55
  192.1 24.0 %all_to_all.82 = f32[4,12,32,192]{3,2,1,0:T(8,128)S(1)} all-to-all(f32[4,12,32,192]{3,2,1,0:T(8,128)S(1)} %bitcast.87), channel_id=1, replica_groups=mesh['cam'=4,'lmk'=32] {'cam'}, dimensions={0} | all-to-all | bytes 2359296 | tf_op jit(solution)/shard_map/all_to_all | solution.py:27
  218.0 15.8 %all_to_all.83 = bf16[4,12,32,192]{3,2,1,0:T(8,128)(2,1)S(1)} all-to-all(bf16[4,12,32,192]{3,2,1,0:T(8,128)(2,1)S(1)} %broadcast_in_dim.37), channel_id=1, replica_groups=mesh['cam'=4,'lmk'=32] {'cam'}, dimensions={0} | all-to-all | bytes 1179648 | tf_op jit(solution)/shard_map/all_to_all | solution.py:20
  234.5 11.3 %subtract_convert_fusion.2 = (bf16[80,32,576]{2,1,0:T(8,128)(2,1)S(1)}, bf16[80,32,576]{2,1,0:T(8,128)(2,1)S(1)}) fusion(bf16[80,576,192]{1,2,0:T(8,128)(2,1)} %param.12, bf16[80,32,192]{2,1,0:T(8,128)(2,1)S(1)} %gather_fusion.3, pred[80]{0:T(512)(128)(4,1)S(1)} %compare_and_fusion), kind=kOutput, calls=%fused_computation.10 | convolution fusion | flops 572620800 | bytes 24576080 | tf_op jit(solution)/shard_map/tpl,tcl->tpc/dot_general | solution.py:68
  250.2 37.3 %all_to_all.84 = f32[32,1,32,576]{3,2,1,0:T(8,128)S(1)} all-to-all(f32[32,1,32,576]{3,2,1,0:T(8,128)S(1)} %copy.54), channel_id=1, replica_groups=mesh['cam'=4,'lmk'=32] {'lmk'}, dimensions={0} | all-to-all | bytes 4718592 | tf_op jit(solution)/shard_map/all_to_all | solution.py:27
  288.7 23.2 %all_to_all.85 = bf16[32,1,32,576]{3,2,1,0:T(8,128)(2,1)S(1)} all-to-all(bf16[32,1,32,576]{3,2,1,0:T(8,128)(2,1)S(1)} %broadcast_in_dim.38), channel_id=1, replica_groups=mesh['cam'=4,'lmk'=32] {'lmk'}, dimensions={0} | all-to-all | bytes 2359296 | tf_op jit(solution)/shard_map/all_to_all | solution.py:20
  311.9 2.9 gather_fusion.4
  314.8 11.5 %subtract_convert_fusion.5 = (bf16[80,32,192]{2,1,0:T(8,128)(2,1)S(1)}, bf16[80,32,192]{2,1,0:T(8,128)(2,1)S(1)}) fusion(bf16[80,576,192]{1,2,0:T(8,128)(2,1)} %param.12, bf16[80,32,576]{2,1,0:T(8,128)(2,1)} %gather_fusion.4, pred[80]{0:T(512)(128)(4,1)S(1)} %compare_and_fusion.1), kind=kOutput, calls=%fused_computation.43 | convolution fusion | flops 569671680 | bytes 22610000 | tf_op jit(solution)/shard_map/tpc,tcl->tpl/dot_general | solution.py:55
  329.2 24.5 %all_to_all.86 = f32[4,12,32,192]{3,2,1,0:T(8,128)S(1)} all-to-all(f32[4,12,32,192]{3,2,1,0:T(8,128)S(1)} %bitcast.88), channel_id=1, replica_groups=mesh['cam'=4,'lmk'=32] {'cam'}, dimensions={0} | all-to-all | bytes 2359296 | tf_op jit(solution)/shard_map/all_to_all | solution.py:27
  355.6 15.7 %all_to_all.87 = bf16[4,12,32,192]{3,2,1,0:T(8,128)(2,1)S(1)} all-to-all(bf16[4,12,32,192]{3,2,1,0:T(8,128)(2,1)S(1)} %broadcast_in_dim.39), channel_id=1, replica_groups=mesh['cam'=4,'lmk'=32] {'cam'}, dimensions={0} | all-to-all | bytes 1179648 | tf_op jit(solution)/shard_map/all_to_all | solution.py:20
  372.0 11.3 %subtract_convert_fusion.1 = (bf16[80,32,576]{2,1,0:T(8,128)(2,1)S(1)}, bf16[80,32,576]{2,1,0:T(8,128)(2,1)S(1)}) fusion(bf16[80,576,192]{1,2,0:T(8,128)(2,1)} %param.12, bf16[80,32,192]{2,1,0:T(8,128)(2,1)S(1)} %gather_fusion.5, pred[80]{0:T(512)(128)(4,1)S(1)} %compare_and_fusion), kind=kOutput, calls=%fused_computation.9 | convolution fusion | flops 572620800 | bytes 24576080 | tf_op jit(solution)/shard_map/tpl,tcl->tpc/dot_general | solution.py:68
  387.7 37.0 %all_to_all.88 = f32[32,1,32,576]{3,2,1,0:T(8,128)S(1)} all-to-all(f32[32,1,32,576]{3,2,1,0:T(8,128)S(1)} %copy.60), channel_id=1, replica_groups=mesh['cam'=4,'lmk'=32] {'lmk'}, dimensions={0} | all-to-all | bytes 4718592 | tf_op jit(solution)/shard_map/all_to_all | solution.py:27
  425.8 23.1 %all_to_all.89 = bf16[32,1,32,576]{3,2,1,0:T(8,128)(2,1)S(1)} all-to-all(bf16[32,1,32,576]{3,2,1,0:T(8,128)(2,1)S(1)} %broadcast_in_dim.40), channel_id=1, replica_groups=mesh['cam'=4,'lmk'=32] {'lmk'}, dimensions={0} | all-to-all | bytes 2359296 | tf_op jit(solution)/shard_map/all_to_all | solution.py:20
  448.9 2.9 gather_fusion.6
  451.8 11.5 %subtract_convert_fusion.4 = (bf16[80,32,192]{2,1,0:T(8,128)(2,1)S(1)}, bf16[80,32,192]{2,1,0:T(8,128)(2,1)S(1)}) fusion(bf16[80,576,192]{1,2,0:T(8,128)(2,1)} %param.12, bf16[80,32,576]{2,1,0:T(8,128)(2,1)} %gather_fusion.6, pred[80]{0:T(512)(128)(4,1)S(1)} %compare_and_fusion.1), kind=kOutput, calls=%fused_computation.41 | convolution fusion | flops 569671680 | bytes 22610000 | tf_op jit(solution)/shard_map/tpc,tcl->tpl/dot_general | solution.py:55
  466.3 24.2 %all_to_all.90 = f32[4,12,32,192]{3,2,1,0:T(8,128)S(1)} all-to-all(f32[4,12,32,192]{3,2,1,0:T(8,128)S(1)} %bitcast.89), channel_id=1, replica_groups=mesh['cam'=4,'lmk'=32] {'cam'}, dimensions={0} | all-to-all | bytes 2359296 | tf_op jit(solution)/shard_map/all_to_all | solution.py:27
  492.3 15.8 %all_to_all.91 = bf16[4,12,32,192]{3,2,1,0:T(8,128)(2,1)S(1)} all-to-all(bf16[4,12,32,192]{3,2,1,0:T(8,128)(2,1)S(1)} %broadcast_in_dim.41), channel_id=1, replica_groups=mesh['cam'=4,'lmk'=32] {'cam'}, dimensions={0} | all-to-all | bytes 1179648 | tf_op jit(solution)/shard_map/all_to_all | solution.py:20
  508.8 11.3 %subtract_convert_fusion = (bf16[80,32,576]{2,1,0:T(8,128)(2,1)S(1)}, bf16[80,32,576]{2,1,0:T(8,128)(2,1)S(1)}) fusion(bf16[80,576,192]{1,2,0:T(8,128)(2,1)} %param.12, bf16[80,32,192]{2,1,0:T(8,128)(2,1)S(1)} %gather_fusion.7, pred[80]{0:T(512)(128)(4,1)S(1)} %compare_and_fusion), kind=kOutput, calls=%fused_computation.8 | convolution fusion | flops 572620800 | bytes 24576080 | tf_op jit(solution)/shard_map/tpl,tcl->tpc/dot_general | solution.py:68
  524.6 37.2 %all_to_all.92 = f32[32,1,32,576]{3,2,1,0:T(8,128)S(1)} all-to-all(f32[32,1,32,576]{3,2,1,0:T(8,128)S(1)} %copy.66), channel_id=1, replica_groups=mesh['cam'=4,'lmk'=32] {'lmk'}, dimensions={0} | all-to-all | bytes 4718592 | tf_op jit(solution)/shard_map/all_to_all | solution.py:27
  (66 shorter events, 49.1 us)
Async XLA Ops:
  0.0 1.1 copy-start
  0.0 12.7 %copy-start.3 = (s32[80]{0:T(128)S(1)}, s32[80]{0:T(128)}, u32[]{:S(2)}) copy-start(s32[80]{0:T(128)} %param.14) | copy-start | bytes 964
  3.9 28.0 %all-to-all-start = ((bf16[32,1,32,576]{3,2,1,0:T(8,128)(2,1)}), bf16[32,1,32,576]{3,2,1,0:T(8,128)(2,1)S(1)}, u32[]{:S(2)}, u32[]{:S(2)}) async-start(bf16[32,1,32,576]{3,2,1,0:T(8,128)(2,1)} %broadcast_in_dim.34), calls=%async_computation | async-start | bytes 2621440 | tf_op jit(solution)/shard_map/all_to_all | solution.py:20
  34.9 11.5 %copy-start.2 = (s32[80]{0:T(128)S(1)}, s32[80]{0:T(128)}, u32[]{:S(2)}) copy-start(s32[80]{0:T(128)} %param.15) | copy-start | bytes 964
  50.5 26.4 %all-to-all-start.1 = ((f32[4,12,32,192]{3,2,1,0:T(8,128)}), f32[4,12,32,192]{3,2,1,0:T(8,128)S(1)}, u32[]{:S(2)}, u32[]{:S(2)}) async-start(f32[4,12,32,192]{3,2,1,0:T(8,128)} %bitcast.86), calls=%async_computation.1 | async-start | bytes 3145728 | tf_op jit(solution)/shard_map/all_to_all | solution.py:27
  79.6 16.7 %all-to-all-start.2 = ((bf16[4,12,32,192]{3,2,1,0:T(8,128)(2,1)}), bf16[4,12,32,192]{3,2,1,0:T(8,128)(2,1)S(1)}, u32[]{:S(2)}, u32[]{:S(2)}) async-start(bf16[4,12,32,192]{3,2,1,0:T(8,128)(2,1)} %broadcast_in_dim.35), calls=%async_computation.2 | async-start | bytes 1572864 | tf_op jit(solution)/shard_map/all_to_all | solution.py:20
  561.7 0.9 copy-start.1

commit v3 on v2

--- a/solution.py
+++ b/solution.py
@@ -24,8 +24,8 @@
 def a2a_reduce_scatter(full, axis_name):
     size = lax.axis_size(axis_name)
     chunks = full.reshape((size, full.shape[0] // size) + full.shape[1:])
-    got = lax.all_to_all(chunks, axis_name, 0, 0, tiled=False)
-    return jnp.sum(got, axis=0)
+    got = lax.all_to_all(chunks.astype(jnp.bfloat16), axis_name, 0, 0, tiled=False)
+    return jnp.sum(got.astype(jnp.float32), axis=0)
 
 
 def a2a_allreduce(full, axis_name):

time: 571 us -> 472 us (0.83)
  blocking collectives: 339 us -> 258 us
  waiting for transfers between devices: 53.8 us -> 45.4 us
  local copies, waits for them, and re-layouts: 29.2 us -> 21.7 us
    all_to_all x7, blocking collectives: 223 us -> 143 us  [a2a_reduce_scatter(): lax.all_to_all(chunks.astype(jnp.bfloat16), axis_name, 0, 0, tiled=False)]
    all_to_all x1, waiting for transfers between devices: 21.6 us -> 13.1 us  [a2a_reduce_scatter(): lax.all_to_all(chunks.astype(jnp.bfloat16), axis_name, 0, 0, tiled=False)]
    reshape x4 -> x0, local copies, waits for them, and re-layouts: 6.09 us -> none  [a2a_reduce_scatter(): chunks = full.reshape((size, full.shape[0] // size) + full.shape[1:])]
where the time goes in v3:
time: 472 us; the launch traced here: 466 us
  blocking collectives  258 us (55%)
  matrix products  121 us (26%)
  waiting for transfers between devices  45.4 us (10%)
  local copies, waits for them, and re-layouts  21.7 us (5%)
  starting transfers between devices  17.3 us (4%)
    all_to_all x7, blocking collectives, a2a_reduce_scatter(): lax.all_to_all(chunks.astype(jnp.bfloat16), axis_name, 0, 0, tiled=False)  143 us
    all_to_all x6, blocking collectives, a2a_gather(): got = lax.all_to_all(tiled, axis_name, 0, 0, tiled=False)  115 us
    dot_general x4, matrix products, local(): jnp.einsum('tpc,tcl->tpl', tile_rows, couplings, preferred_element_type=j...  46.1 us
    dot_general x4, matrix products, local(): jnp.einsum('tpl,tcl->tpc', picked, couplings, preferred_element_type=jnp....  45 us
    all_to_all x2, waiting for transfers between devices, a2a_gather(): got = lax.all_to_all(tiled, axis_name, 0, 0, tiled=False)  32.2 us
    all_to_all x1, waiting for transfers between devices, a2a_reduce_scatter(): lax.all_to_all(chunks.astype(jnp.bfloat16), axis_name, 0, 0, tiled=False)  13.1 us
    all_to_all x2, starting transfers between devices, a2a_gather(): got = lax.all_to_all(tiled, axis_name, 0, 0, tiled=False)  12.4 us
    gather x4, local copies, waits for them, and re-layouts, local(): tile_rows = jnp.take(panel, tile_cam, axis=0)  11.6 us
  transfers between devices with their start and end apart: 3, of which 3 were waited for; matrix products, arithmetic and copies ran while one was open for 0% of the time, Pallas kernels for 0%

profile of v3, /device:TPU:0, one launch (start us, length us, event | category | flops | bytes accessed | tf_op | source)
XLA Modules:
  0.0 465.9 jit_solution(17587452913749692988)
XLA Ops:
  3.9 8.8 %all-to-all-start = ((bf16[32,1,32,576]{3,2,1,0:T(8,128)(2,1)}), bf16[32,1,32,576]{3,2,1,0:T(8,128)(2,1)S(1)}, u32[]{:S(2)}, u32[]{:S(2)}) async-start(bf16[32,1,32,576]{3,2,1,0:T(8,128)(2,1)} %broadcast_in_dim.34), calls=%async_computation | async-start | bytes 2621440 | tf_op jit(solution)/shard_map/all_to_all | solution.py:20
  12.8 19.2 %all-to-all-done = bf16[32,1,32,576]{3,2,1,0:T(8,128)(2,1)S(1)} async-done(((bf16[32,1,32,576]{3,2,1,0:T(8,128)(2,1)}), bf16[32,1,32,576]{3,2,1,0:T(8,128)(2,1)S(1)}, u32[]{:S(2)}, u32[]{:S(2)}) %all-to-all-start) | async-done | bytes 1179680 | tf_op jit(solution)/shard_map/all_to_all | solution.py:20
  32.0 2.9 gather_fusion
  34.9 11.5 %subtract_convert_fusion.7 = (bf16[80,32,192]{2,1,0:T(8,128)(2,1)S(1)}, bf16[80,32,192]{2,1,0:T(8,128)(2,1)S(1)}) fusion(bf16[80,576,192]{1,2,0:T(8,128)(2,1)} %param.12, bf16[80,32,576]{2,1,0:T(8,128)(2,1)} %gather_fusion, pred[80]{0:T(512)(128)(4,1)S(1)} %compare_and_fusion.1), kind=kOutput, calls=%fused_computation.47 | convolution fusion | flops 569671680 | bytes 22610000 | tf_op jit(solution)/shard_map/tpc,tcl->tpl/dot_general | solution.py:55
  49.6 4.9 %all-to-all-start.1 = ((bf16[4,12,32,192]{3,2,1,0:T(8,128)(2,1)}), bf16[4,12,32,192]{3,2,1,0:T(8,128)(2,1)S(1)}, u32[]{:S(2)}, u32[]{:S(2)}) async-start(bf16[4,12,32,192]{3,2,1,0:T(8,128)(2,1)} %bitcast.5), calls=%async_computation.1 | async-start | bytes 1572864 | tf_op jit(solution)/shard_map/all_to_all | solution.py:27
  54.4 13.1 %all-to-all-done.1 = bf16[4,12,32,192]{3,2,1,0:T(8,128)(2,1)S(1)} async-done(((bf16[4,12,32,192]{3,2,1,0:T(8,128)(2,1)}), bf16[4,12,32,192]{3,2,1,0:T(8,128)(2,1)S(1)}, u32[]{:S(2)}, u32[]{:S(2)}) %all-to-all-start.1) | async-done | bytes 589856 | tf_op jit(solution)/shard_map/all_to_all | solution.py:27
  70.3 3.7 all-to-all-start.2
  74.0 13.0 %all-to-all-done.2 = bf16[4,12,32,192]{3,2,1,0:T(8,128)(2,1)S(1)} async-done(((bf16[4,12,32,192]{3,2,1,0:T(8,128)(2,1)}), bf16[4,12,32,192]{3,2,1,0:T(8,128)(2,1)S(1)}, u32[]{:S(2)}, u32[]{:S(2)}) %all-to-all-start.2) | async-done | bytes 589856 | tf_op jit(solution)/shard_map/all_to_all | solution.py:20
  87.7 11.3 %subtract_convert_fusion.3 = (bf16[80,32,576]{2,1,0:T(8,128)(2,1)S(1)}, bf16[80,32,576]{2,1,0:T(8,128)(2,1)S(1)}) fusion(bf16[80,576,192]{1,2,0:T(8,128)(2,1)} %param.12, bf16[80,32,192]{2,1,0:T(8,128)(2,1)S(1)} %gather_fusion.1, pred[80]{0:T(512)(128)(4,1)S(1)} %compare_and_fusion), kind=kOutput, calls=%fused_computation.11 | convolution fusion | flops 572620800 | bytes 24576080 | tf_op jit(solution)/shard_map/tpl,tcl->tpc/dot_general | solution.py:68
  102.5 24.9 %all_to_all.80 = bf16[32,1,32,576]{3,2,1,0:T(8,128)(2,1)S(1)} all-to-all(bf16[32,1,32,576]{3,2,1,0:T(8,128)(2,1)S(1)} %copy.48), channel_id=1, replica_groups=mesh['cam'=4,'lmk'=32] {'lmk'}, dimensions={0} | all-to-all | bytes 2359296 | tf_op jit(solution)/shard_map/all_to_all | solution.py:27
  127.9 22.9 %all_to_all.81 = bf16[32,1,32,576]{3,2,1,0:T(8,128)(2,1)S(1)} all-to-all(bf16[32,1,32,576]{3,2,1,0:T(8,128)(2,1)S(1)} %broadcast_in_dim.36), channel_id=1, replica_groups=mesh['cam'=4,'lmk'=32] {'lmk'}, dimensions={0} | all-to-all | bytes 2359296 | tf_op jit(solution)/shard_map/all_to_all | solution.py:20
  150.9 2.9 gather_fusion.2
  153.8 11.5 %subtract_convert_fusion.6 = (bf16[80,32,192]{2,1,0:T(8,128)(2,1)S(1)}, bf16[80,32,192]{2,1,0:T(8,128)(2,1)S(1)}) fusion(bf16[80,576,192]{1,2,0:T(8,128)(2,1)} %param.12, bf16[80,32,576]{2,1,0:T(8,128)(2,1)} %gather_fusion.2, pred[80]{0:T(512)(128)(4,1)S(1)} %compare_and_fusion.1), kind=kOutput, calls=%fused_computation.45 | convolution fusion | flops 569671680 | bytes 22610000 | tf_op jit(solution)/shard_map/tpc,tcl->tpl/dot_general | solution.py:55
  167.6 15.5 %all_to_all.82 = bf16[4,12,32,192]{3,2,1,0:T(8,128)(2,1)S(1)} all-to-all(bf16[4,12,32,192]{3,2,1,0:T(8,128)(2,1)S(1)} %bitcast.90), channel_id=1, replica_groups=mesh['cam'=4,'lmk'=32] {'cam'}, dimensions={0} | all-to-all | bytes 1179648 | tf_op jit(solution)/shard_map/all_to_all | solution.py:27
  185.0 15.5 %all_to_all.83 = bf16[4,12,32,192]{3,2,1,0:T(8,128)(2,1)S(1)} all-to-all(bf16[4,12,32,192]{3,2,1,0:T(8,128)(2,1)S(1)} %broadcast_in_dim.37), channel_id=1, replica_groups=mesh['cam'=4,'lmk'=32] {'cam'}, dimensions={0} | all-to-all | bytes 1179648 | tf_op jit(solution)/shard_map/all_to_all | solution.py:20
  201.2 11.3 %subtract_convert_fusion.2 = (bf16[80,32,576]{2,1,0:T(8,128)(2,1)S(1)}, bf16[80,32,576]{2,1,0:T(8,128)(2,1)S(1)}) fusion(bf16[80,576,192]{1,2,0:T(8,128)(2,1)} %param.12, bf16[80,32,192]{2,1,0:T(8,128)(2,1)S(1)} %gather_fusion.3, pred[80]{0:T(512)(128)(4,1)S(1)} %compare_and_fusion), kind=kOutput, calls=%fused_computation.10 | convolution fusion | flops 572620800 | bytes 24576080 | tf_op jit(solution)/shard_map/tpl,tcl->tpc/dot_general | solution.py:68
  216.0 24.2 %all_to_all.84 = bf16[32,1,32,576]{3,2,1,0:T(8,128)(2,1)S(1)} all-to-all(bf16[32,1,32,576]{3,2,1,0:T(8,128)(2,1)S(1)} %copy.54), channel_id=1, replica_groups=mesh['cam'=4,'lmk'=32] {'lmk'}, dimensions={0} | all-to-all | bytes 2359296 | tf_op jit(solution)/shard_map/all_to_all | solution.py:27
  240.7 22.6 %all_to_all.85 = bf16[32,1,32,576]{3,2,1,0:T(8,128)(2,1)S(1)} all-to-all(bf16[32,1,32,576]{3,2,1,0:T(8,128)(2,1)S(1)} %broadcast_in_dim.38), channel_id=1, replica_groups=mesh['cam'=4,'lmk'=32] {'lmk'}, dimensions={0} | all-to-all | bytes 2359296 | tf_op jit(solution)/shard_map/all_to_all | solution.py:20
  263.4 2.9 gather_fusion.4
  266.3 11.5 %subtract_convert_fusion.5 = (bf16[80,32,192]{2,1,0:T(8,128)(2,1)S(1)}, bf16[80,32,192]{2,1,0:T(8,128)(2,1)S(1)}) fusion(bf16[80,576,192]{1,2,0:T(8,128)(2,1)} %param.12, bf16[80,32,576]{2,1,0:T(8,128)(2,1)} %gather_fusion.4, pred[80]{0:T(512)(128)(4,1)S(1)} %compare_and_fusion.1), kind=kOutput, calls=%fused_computation.43 | convolution fusion | flops 569671680 | bytes 22610000 | tf_op jit(solution)/shard_map/tpc,tcl->tpl/dot_general | solution.py:55
  280.1 15.9 %all_to_all.86 = bf16[4,12,32,192]{3,2,1,0:T(8,128)(2,1)S(1)} all-to-all(bf16[4,12,32,192]{3,2,1,0:T(8,128)(2,1)S(1)} %bitcast.91), channel_id=1, replica_groups=mesh['cam'=4,'lmk'=32] {'cam'}, dimensions={0} | all-to-all | bytes 1179648 | tf_op jit(solution)/shard_map/all_to_all | solution.py:27
  297.8 15.5 %all_to_all.87 = bf16[4,12,32,192]{3,2,1,0:T(8,128)(2,1)S(1)} all-to-all(bf16[4,12,32,192]{3,2,1,0:T(8,128)(2,1)S(1)} %broadcast_in_dim.39), channel_id=1, replica_groups=mesh['cam'=4,'lmk'=32] {'cam'}, dimensions={0} | all-to-all | bytes 1179648 | tf_op jit(solution)/shard_map/all_to_all | solution.py:20
  314.1 11.3 %subtract_convert_fusion.1 = (bf16[80,32,576]{2,1,0:T(8,128)(2,1)S(1)}, bf16[80,32,576]{2,1,0:T(8,128)(2,1)S(1)}) fusion(bf16[80,576,192]{1,2,0:T(8,128)(2,1)} %param.12, bf16[80,32,192]{2,1,0:T(8,128)(2,1)S(1)} %gather_fusion.5, pred[80]{0:T(512)(128)(4,1)S(1)} %compare_and_fusion), kind=kOutput, calls=%fused_computation.9 | convolution fusion | flops 572620800 | bytes 24576080 | tf_op jit(solution)/shard_map/tpl,tcl->tpc/dot_general | solution.py:68
  328.9 23.4 %all_to_all.88 = bf16[32,1,32,576]{3,2,1,0:T(8,128)(2,1)S(1)} all-to-all(bf16[32,1,32,576]{3,2,1,0:T(8,128)(2,1)S(1)} %copy.60), channel_id=1, replica_groups=mesh['cam'=4,'lmk'=32] {'lmk'}, dimensions={0} | all-to-all | bytes 2359296 | tf_op jit(solution)/shard_map/all_to_all | solution.py:27
  352.8 22.8 %all_to_all.89 = bf16[32,1,32,576]{3,2,1,0:T(8,128)(2,1)S(1)} all-to-all(bf16[32,1,32,576]{3,2,1,0:T(8,128)(2,1)S(1)} %broadcast_in_dim.40), channel_id=1, replica_groups=mesh['cam'=4,'lmk'=32] {'lmk'}, dimensions={0} | all-to-all | bytes 2359296 | tf_op jit(solution)/shard_map/all_to_all | solution.py:20
  375.6 2.9 gather_fusion.6
  378.5 11.5 %subtract_convert_fusion.4 = (bf16[80,32,192]{2,1,0:T(8,128)(2,1)S(1)}, bf16[80,32,192]{2,1,0:T(8,128)(2,1)S(1)}) fusion(bf16[80,576,192]{1,2,0:T(8,128)(2,1)} %param.12, bf16[80,32,576]{2,1,0:T(8,128)(2,1)} %gather_fusion.6, pred[80]{0:T(512)(128)(4,1)S(1)} %compare_and_fusion.1), kind=kOutput, calls=%fused_computation.41 | convolution fusion | flops 569671680 | bytes 22610000 | tf_op jit(solution)/shard_map/tpc,tcl->tpl/dot_general | solution.py:55
  392.3 15.9 %all_to_all.90 = bf16[4,12,32,192]{3,2,1,0:T(8,128)(2,1)S(1)} all-to-all(bf16[4,12,32,192]{3,2,1,0:T(8,128)(2,1)S(1)} %bitcast.92), channel_id=1, replica_groups=mesh['cam'=4,'lmk'=32] {'cam'}, dimensions={0} | all-to-all | bytes 1179648 | tf_op jit(solution)/shard_map/all_to_all | solution.py:27
  410.0 15.5 %all_to_all.91 = bf16[4,12,32,192]{3,2,1,0:T(8,128)(2,1)S(1)} all-to-all(bf16[4,12,32,192]{3,2,1,0:T(8,128)(2,1)S(1)} %broadcast_in_dim.41), channel_id=1, replica_groups=mesh['cam'=4,'lmk'=32] {'cam'}, dimensions={0} | all-to-all | bytes 1179648 | tf_op jit(solution)/shard_map/all_to_all | solution.py:20
  426.2 11.3 %subtract_convert_fusion = (bf16[80,32,576]{2,1,0:T(8,128)(2,1)S(1)}, bf16[80,32,576]{2,1,0:T(8,128)(2,1)S(1)}) fusion(bf16[80,576,192]{1,2,0:T(8,128)(2,1)} %param.12, bf16[80,32,192]{2,1,0:T(8,128)(2,1)S(1)} %gather_fusion.7, pred[80]{0:T(512)(128)(4,1)S(1)} %compare_and_fusion), kind=kOutput, calls=%fused_computation.8 | convolution fusion | flops 572620800 | bytes 24576080 | tf_op jit(solution)/shard_map/tpl,tcl->tpc/dot_general | solution.py:68
  439.0 1.7 fusion.49
  441.1 23.5 %all_to_all.92 = bf16[32,1,32,576]{3,2,1,0:T(8,128)(2,1)S(1)} all-to-all(bf16[32,1,32,576]{3,2,1,0:T(8,128)(2,1)S(1)} %copy.66), channel_id=1, replica_groups=mesh['cam'=4,'lmk'=32] {'lmk'}, dimensions={0} | all-to-all | bytes 2359296 | tf_op jit(solution)/shard_map/all_to_all | solution.py:27
  (66 shorter events, 40.1 us)
Async XLA Ops:
  0.0 1.1 copy-start
  0.0 12.7 %copy-start.2 = (s32[80]{0:T(128)S(1)}, s32[80]{0:T(128)}, u32[]{:S(2)}) copy-start(s32[80]{0:T(128)} %param.14) | copy-start | bytes 964
  3.9 28.0 %all-to-all-start = ((bf16[32,1,32,576]{3,2,1,0:T(8,128)(2,1)}), bf16[32,1,32,576]{3,2,1,0:T(8,128)(2,1)S(1)}, u32[]{:S(2)}, u32[]{:S(2)}) async-start(bf16[32,1,32,576]{3,2,1,0:T(8,128)(2,1)} %broadcast_in_dim.34), calls=%async_computation | async-start | bytes 2621440 | tf_op jit(solution)/shard_map/all_to_all | solution.py:20
  34.9 11.5 %copy-start.3 = (s32[80]{0:T(128)S(1)}, s32[80]{0:T(128)}, u32[]{:S(2)}) copy-start(s32[80]{0:T(128)} %param.15) | copy-start | bytes 964
  49.6 18.0 %all-to-all-start.1 = ((bf16[4,12,32,192]{3,2,1,0:T(8,128)(2,1)}), bf16[4,12,32,192]{3,2,1,0:T(8,128)(2,1)S(1)}, u32[]{:S(2)}, u32[]{:S(2)}) async-start(bf16[4,12,32,192]{3,2,1,0:T(8,128)(2,1)} %bitcast.5), calls=%async_computation.1 | async-start | bytes 1572864 | tf_op jit(solution)/shard_map/all_to_all | solution.py:27
  70.3 16.7 %all-to-all-start.2 = ((bf16[4,12,32,192]{3,2,1,0:T(8,128)(2,1)}), bf16[4,12,32,192]{3,2,1,0:T(8,128)(2,1)S(1)}, u32[]{:S(2)}, u32[]{:S(2)}) async-start(bf16[4,12,32,192]{3,2,1,0:T(8,128)(2,1)} %broadcast_in_dim.35), calls=%async_computation.2 | async-start | bytes 1572864 | tf_op jit(solution)/shard_map/all_to_all | solution.py:20
  441.1 23.7 %copy-start.1 = (f32[32,576]{1,0:T(8,128)S(1)}, f32[32,576]{1,0:T(8,128)}, u32[]{:S(2)}) copy-start(f32[32,576]{1,0:T(8,128)} %get-tuple-element.24) | copy-start | bytes 221188

commit v4 on v3

--- a/solution.py
+++ b/solution.py
@@ -1,9 +1,77 @@
+import functools
+
 import jax
 import jax.numpy as jnp
 from jax import lax
+from jax.experimental import pallas as pl
+from jax.experimental.pallas import tpu as pltpu
 from jax.sharding import PartitionSpec as P
 
 POWERS = 4
+MESH = pl.DeviceIdType.MESH
+AXES = ("cam", "lmk")
+COLLECTIVE_IDS = {}
+
+
+def exchange_kernel(n, axis, x_ref, o_ref, send_sem, recv_sem, local_sem):
+    me = lax.axis_index(axis)
+    coords = tuple(lax.axis_index(name) for name in AXES)
+    slot = AXES.index(axis)
+
+    def device(peer):
+        return coords[:slot] + (peer,) + coords[slot + 1:]
+
+    barrier = pltpu.get_barrier_semaphore()
+    for step in range(1, n):
+        pl.semaphore_signal(barrier, inc=1, device_id=device(lax.rem(me + step, n)), device_id_type=MESH)
+    pl.semaphore_wait(barrier, n - 1)
+    local = pltpu.make_async_copy(x_ref.at[me], o_ref.at[me], local_sem)
+    local.start()
+    sends = []
+    for step in range(1, n):
+        peer = lax.rem(me + step, n)
+        copy = pltpu.make_async_remote_copy(
+            src_ref=x_ref.at[peer],
+            dst_ref=o_ref.at[me],
+            send_sem=send_sem.at[step],
+            recv_sem=recv_sem.at[step],
+            device_id=device(peer),
+            device_id_type=MESH,
+        )
+        copy.start()
+        sends.append(copy)
+    local.wait()
+    for copy in sends:
+        copy.wait_send()
+    for step in range(1, n):
+        source = lax.rem(me + n - step, n)
+        pltpu.make_async_remote_copy(
+            src_ref=x_ref.at[source],
+            dst_ref=o_ref.at[source],
+            send_sem=send_sem.at[step],
+            recv_sem=recv_sem.at[step],
+            device_id=device(source),
+            device_id_type=MESH,
+        ).wait_recv()
+
+
+def exchange(x, axis_name):
+    n = lax.axis_size(axis_name)
+    key = (axis_name, x.shape, str(x.dtype))
+    if key not in COLLECTIVE_IDS:
+        COLLECTIVE_IDS[key] = len(COLLECTIVE_IDS)
+    return pl.pallas_call(
+        functools.partial(exchange_kernel, n, axis_name),
+        out_shape=jax.ShapeDtypeStruct(x.shape, x.dtype),
+        in_specs=[pl.BlockSpec(memory_space=pl.ANY)],
+        out_specs=pl.BlockSpec(memory_space=pl.ANY),
+        scratch_shapes=[
+            pltpu.SemaphoreType.DMA((n,)),
+            pltpu.SemaphoreType.DMA((n,)),
+            pltpu.SemaphoreType.DMA,
+        ],
+        compiler_params=pltpu.CompilerParams(collective_id=COLLECTIVE_IDS[key], has_side_effects=True),
+    )(x)
 
 
 def onehot_sum(selected, values):
@@ -17,21 +85,21 @@
 def a2a_gather(block, axis_name):
     size = lax.axis_size(axis_name)
     tiled = jnp.broadcast_to(block[None], (size,) + block.shape)
-    got = lax.all_to_all(tiled, axis_name, 0, 0, tiled=False)
+    got = exchange(tiled, axis_name)
     return got.reshape((size * block.shape[0],) + block.shape[1:])
 
 
 def a2a_reduce_scatter(full, axis_name):
     size = lax.axis_size(axis_name)
     chunks = full.reshape((size, full.shape[0] // size) + full.shape[1:])
-    got = lax.all_to_all(chunks.astype(jnp.bfloat16), axis_name, 0, 0, tiled=False)
+    got = exchange(chunks.astype(jnp.bfloat16), axis_name)
     return jnp.sum(got.astype(jnp.float32), axis=0)
 
 
 def a2a_allreduce(full, axis_name):
     size = lax.axis_size(axis_name)
     tiled = jnp.broadcast_to(full[None], (size,) + full.shape)
-    got = lax.all_to_all(tiled, axis_name, 0, 0, tiled=False)
+    got = exchange(tiled, axis_name)
     return jnp.sum(got, axis=0)
 
 
@@ -80,6 +148,7 @@
 
 
 def solution(mesh):
+    COLLECTIVE_IDS.clear()
     in_specs = (
         P(("cam", "lmk"), None, None),
         P(("cam", "lmk"), None, None),

time: 472 us -> 487 us (1.032)
  Pallas kernels: 0 us -> 292 us
  blocking collectives: 258 us -> 0 us
  waiting for transfers between devices: 45.4 us -> 0 us
  other arithmetic: 1.47 us -> 29.9 us
  starting transfers between devices: 17.3 us -> 0 us
  local copies, waits for them, and re-layouts: 21.7 us -> 37.2 us
    pallas_call x0 -> x16, Pallas kernels: none -> 292 us  [exchange(): pl.pallas_call(functools.partial(exchange_kernel, n, axis_name), out_shap...]
    all_to_all x13 -> x0, blocking collectives: 258 us -> none  [the longest x7 143 us: a2a_reduce_scatter(): lax.all_to_all(chunks.astype(jnp.bfloat16), axis_name, 0, 0, tiled=False)]
    all_to_all x3 -> x0, waiting for transfers between devices: 45.4 us -> none  [the longest x2 32.2 us: a2a_gather(): got = lax.all_to_all(tiled, axis_name, 0, 0, tiled=False)]
    all_to_all x3 -> x0, starting transfers between devices: 17.3 us -> none  [the longest x2 12.4 us: a2a_gather(): got = lax.all_to_all(tiled, axis_name, 0, 0, tiled=False)]
    convert_element_type x0 -> x4, other arithmetic: none -> 15.5 us  [a2a_reduce_scatter(): got = exchange(chunks.astype(jnp.bfloat16), axis_name)]
    reduce_sum x8, other arithmetic: 1.43 us -> 11.7 us  [a2a_reduce_scatter(): return jnp.sum(got.astype(jnp.float32), axis=0)]
    broadcast_in_dim x8, local copies, waits for them, and re-layouts: 2.72 us -> 8.57 us  [a2a_gather(): tiled = jnp.broadcast_to(block[None], (size,) + block.shape)]
    gather x4, local copies, waits for them, and re-layouts: 11.6 us -> 16.9 us  [local(): tile_rows = jnp.take(panel, tile_cam, axis=0)]
  transfers between devices with their start and end apart: 3 -> 0, of which waited for: 3 -> 0; matrix products, arithmetic and copies ran while one was open for 0% -> 0% of each run, Pallas kernels for 0% -> 0%
where the time goes in v4:
time: 487 us; the launch traced here: 481 us
  Pallas kernels  292 us (60%)
  matrix products  121 us (25%)
  local copies, waits for them, and re-layouts  37.2 us (8%)
  other arithmetic  29.9 us (6%)
    pallas_call x16, Pallas kernels, exchange(): pl.pallas_call(functools.partial(exchange_kernel, n, axis_name), out_shap...  292 us
    dot_general x4, matrix products, local(): jnp.einsum('tpc,tcl->tpl', tile_rows, couplings, preferred_element_type=j...  46.3 us
    dot_general x4, matrix products, local(): jnp.einsum('tpl,tcl->tpc', picked, couplings, preferred_element_type=jnp....  45 us
    gather x4, local copies, waits for them, and re-layouts, local(): tile_rows = jnp.take(panel, tile_cam, axis=0)  16.9 us
    convert_element_type x4, other arithmetic, a2a_reduce_scatter(): got = exchange(chunks.astype(jnp.bfloat16), axis_name)  15.5 us
    reduce_sum x8, other arithmetic, a2a_reduce_scatter(): return jnp.sum(got.astype(jnp.float32), axis=0)  11.7 us
    dot_general x8, matrix products, onehot_sum(): jnp.einsum('st,tpx->spx', selected, lower, preferred_element_type=jnp.flo...  9.98 us
    dot_general x8, matrix products, onehot_sum(): jnp.einsum('st,tpx->spx', selected, upper, preferred_element_type=jnp.flo...  9.79 us

profile of v4, /device:TPU:0, one launch (start us, length us, event | category | flops | bytes accessed | tf_op | source)
XLA Modules:
  0.0 481.2 jit_solution(990439659106166528)
XLA Ops:
  5.6 25.3 %shard_map.64 = bf16[32,1,32,576]{3,2,1,0:T(8,128)(2,1)} custom-call(bf16[32,1,32,576]{3,2,1,0:T(8,128)(2,1)} %broadcast_in_dim.34.x_ref), custom_call_target="tpu_custom_call" | custom-call | tf_op jit(solution)/shard_map/pallas_call | solution.py:63
  30.9 4.2 gather_fusion
  35.1 11.7 %subtract_convert_fusion.7 = (bf16[80,32,192]{2,1,0:T(8,128)(2,1)S(1)}, bf16[80,32,192]{2,1,0:T(8,128)(2,1)S(1)}) fusion(bf16[80,576,192]{1,2,0:T(8,128)(2,1)} %param.12, bf16[80,32,576]{2,1,0:T(8,128)(2,1)} %gather_fusion, pred[80]{0:T(512)(128)(4,1)S(1)} %compare_and_fusion.1), kind=kOutput, calls=%fused_computation.51 | convolution fusion | flops 569671680 | bytes 22610000 | tf_op jit(solution)/shard_map/tpc,tcl->tpl/dot_general | solution.py:123
  50.0 12.9 %shard_map.65 = bf16[4,12,32,192]{3,2,1,0:T(8,128)(2,1)} custom-call(bf16[4,12,32,192]{3,2,1,0:T(8,128)(2,1)} %bitcast.90), custom_call_target="tpu_custom_call" | custom-call | tf_op jit(solution)/shard_map/pallas_call | solution.py:63
  66.8 12.7 %shard_map.66 = bf16[4,12,32,192]{3,2,1,0:T(8,128)(2,1)} custom-call(bf16[4,12,32,192]{3,2,1,0:T(8,128)(2,1)} %broadcast_in_dim.35.x_ref), custom_call_target="tpu_custom_call" | custom-call | tf_op jit(solution)/shard_map/pallas_call | solution.py:63
  81.4 11.3 %subtract_convert_fusion.3 = (bf16[80,32,576]{2,1,0:T(8,128)(2,1)S(1)}, bf16[80,32,576]{2,1,0:T(8,128)(2,1)S(1)}) fusion(bf16[80,576,192]{1,2,0:T(8,128)(2,1)} %param.12, bf16[80,32,192]{2,1,0:T(8,128)(2,1)S(1)} %gather_fusion.1, pred[80]{0:T(512)(128)(4,1)S(1)} %compare_and_fusion), kind=kOutput, calls=%fused_computation.11 | convolution fusion | flops 572620800 | bytes 24576080 | tf_op jit(solution)/shard_map/tpl,tcl->tpc/dot_general | solution.py:136
  95.6 3.9 fusion.36.x_ref
  99.4 24.9 %shard_map.67 = bf16[32,1,32,576]{3,2,1,0:T(8,128)(2,1)} custom-call(bf16[32,1,32,576]{3,2,1,0:T(8,128)(2,1)} %fusion.36.x_ref), custom_call_target="tpu_custom_call" | custom-call | tf_op jit(solution)/shard_map/pallas_call | solution.py:63
  127.7 23.6 %shard_map.68 = bf16[32,1,32,576]{3,2,1,0:T(8,128)(2,1)} custom-call(bf16[32,1,32,576]{3,2,1,0:T(8,128)(2,1)} %broadcast_in_dim.36.x_ref), custom_call_target="tpu_custom_call" | custom-call | tf_op jit(solution)/shard_map/pallas_call | solution.py:63
  151.3 4.2 gather_fusion.2
  155.5 11.5 %subtract_convert_fusion.6 = (bf16[80,32,192]{2,1,0:T(8,128)(2,1)S(1)}, bf16[80,32,192]{2,1,0:T(8,128)(2,1)S(1)}) fusion(bf16[80,576,192]{1,2,0:T(8,128)(2,1)} %param.12, bf16[80,32,576]{2,1,0:T(8,128)(2,1)} %gather_fusion.2, pred[80]{0:T(512)(128)(4,1)S(1)} %compare_and_fusion.1), kind=kOutput, calls=%fused_computation.50 | convolution fusion | flops 569671680 | bytes 22610000 | tf_op jit(solution)/shard_map/tpc,tcl->tpl/dot_general | solution.py:123
  170.2 9.7 %shard_map.69 = bf16[4,12,32,192]{3,2,1,0:T(8,128)(2,1)} custom-call(bf16[4,12,32,192]{3,2,1,0:T(8,128)(2,1)} %bitcast.91), custom_call_target="tpu_custom_call" | custom-call | tf_op jit(solution)/shard_map/pallas_call | solution.py:63
  183.8 12.7 %shard_map.70 = bf16[4,12,32,192]{3,2,1,0:T(8,128)(2,1)} custom-call(bf16[4,12,32,192]{3,2,1,0:T(8,128)(2,1)} %broadcast_in_dim.37.x_ref), custom_call_target="tpu_custom_call" | custom-call | tf_op jit(solution)/shard_map/pallas_call | solution.py:63
  198.4 11.3 %subtract_convert_fusion.2 = (bf16[80,32,576]{2,1,0:T(8,128)(2,1)S(1)}, bf16[80,32,576]{2,1,0:T(8,128)(2,1)S(1)}) fusion(bf16[80,576,192]{1,2,0:T(8,128)(2,1)} %param.12, bf16[80,32,192]{2,1,0:T(8,128)(2,1)S(1)} %gather_fusion.3, pred[80]{0:T(512)(128)(4,1)S(1)} %compare_and_fusion), kind=kOutput, calls=%fused_computation.10 | convolution fusion | flops 572620800 | bytes 24576080 | tf_op jit(solution)/shard_map/tpl,tcl->tpc/dot_general | solution.py:136
  212.6 3.9 fusion.37.x_ref
  216.4 24.6 %shard_map.71 = bf16[32,1,32,576]{3,2,1,0:T(8,128)(2,1)} custom-call(bf16[32,1,32,576]{3,2,1,0:T(8,128)(2,1)} %fusion.37.x_ref), custom_call_target="tpu_custom_call" | custom-call | tf_op jit(solution)/shard_map/pallas_call | solution.py:63
  244.1 23.6 %shard_map.72 = bf16[32,1,32,576]{3,2,1,0:T(8,128)(2,1)} custom-call(bf16[32,1,32,576]{3,2,1,0:T(8,128)(2,1)} %broadcast_in_dim.38.x_ref), custom_call_target="tpu_custom_call" | custom-call | tf_op jit(solution)/shard_map/pallas_call | solution.py:63
  267.7 4.2 gather_fusion.4
  271.9 11.5 %subtract_convert_fusion.5 = (bf16[80,32,192]{2,1,0:T(8,128)(2,1)S(1)}, bf16[80,32,192]{2,1,0:T(8,128)(2,1)S(1)}) fusion(bf16[80,576,192]{1,2,0:T(8,128)(2,1)} %param.12, bf16[80,32,576]{2,1,0:T(8,128)(2,1)} %gather_fusion.4, pred[80]{0:T(512)(128)(4,1)S(1)} %compare_and_fusion.1), kind=kOutput, calls=%fused_computation.49 | convolution fusion | flops 569671680 | bytes 22610000 | tf_op jit(solution)/shard_map/tpc,tcl->tpl/dot_general | solution.py:123
  286.6 14.1 %shard_map.73 = bf16[4,12,32,192]{3,2,1,0:T(8,128)(2,1)} custom-call(bf16[4,12,32,192]{3,2,1,0:T(8,128)(2,1)} %bitcast.92), custom_call_target="tpu_custom_call" | custom-call | tf_op jit(solution)/shard_map/pallas_call | solution.py:63
  304.6 12.7 %shard_map.74 = bf16[4,12,32,192]{3,2,1,0:T(8,128)(2,1)} custom-call(bf16[4,12,32,192]{3,2,1,0:T(8,128)(2,1)} %broadcast_in_dim.39.x_ref), custom_call_target="tpu_custom_call" | custom-call | tf_op jit(solution)/shard_map/pallas_call | solution.py:63
  319.2 11.3 %subtract_convert_fusion.1 = (bf16[80,32,576]{2,1,0:T(8,128)(2,1)S(1)}, bf16[80,32,576]{2,1,0:T(8,128)(2,1)S(1)}) fusion(bf16[80,576,192]{1,2,0:T(8,128)(2,1)} %param.12, bf16[80,32,192]{2,1,0:T(8,128)(2,1)S(1)} %gather_fusion.5, pred[80]{0:T(512)(128)(4,1)S(1)} %compare_and_fusion), kind=kOutput, calls=%fused_computation.9 | convolution fusion | flops 572620800 | bytes 24576080 | tf_op jit(solution)/shard_map/tpl,tcl->tpc/dot_general | solution.py:136
  333.3 3.9 fusion.38.x_ref
  337.2 25.5 %shard_map.75 = bf16[32,1,32,576]{3,2,1,0:T(8,128)(2,1)} custom-call(bf16[32,1,32,576]{3,2,1,0:T(8,128)(2,1)} %fusion.38.x_ref), custom_call_target="tpu_custom_call" | custom-call | tf_op jit(solution)/shard_map/pallas_call | solution.py:63
  365.8 23.0 %shard_map.76 = bf16[32,1,32,576]{3,2,1,0:T(8,128)(2,1)} custom-call(bf16[32,1,32,576]{3,2,1,0:T(8,128)(2,1)} %broadcast_in_dim.40.x_ref), custom_call_target="tpu_custom_call" | custom-call | tf_op jit(solution)/shard_map/pallas_call | solution.py:63
  388.9 4.2 gather_fusion.6
  393.1 11.5 %subtract_convert_fusion.4 = (bf16[80,32,192]{2,1,0:T(8,128)(2,1)S(1)}, bf16[80,32,192]{2,1,0:T(8,128)(2,1)S(1)}) fusion(bf16[80,576,192]{1,2,0:T(8,128)(2,1)} %param.12, bf16[80,32,576]{2,1,0:T(8,128)(2,1)} %gather_fusion.6, pred[80]{0:T(512)(128)(4,1)S(1)} %compare_and_fusion.1), kind=kOutput, calls=%fused_computation.48 | convolution fusion | flops 569671680 | bytes 22610000 | tf_op jit(solution)/shard_map/tpc,tcl->tpl/dot_general | solution.py:123
  407.8 9.7 %shard_map.77 = bf16[4,12,32,192]{3,2,1,0:T(8,128)(2,1)} custom-call(bf16[4,12,32,192]{3,2,1,0:T(8,128)(2,1)} %bitcast.93), custom_call_target="tpu_custom_call" | custom-call | tf_op jit(solution)/shard_map/pallas_call | solution.py:63
  421.4 12.7 %shard_map.78 = bf16[4,12,32,192]{3,2,1,0:T(8,128)(2,1)} custom-call(bf16[4,12,32,192]{3,2,1,0:T(8,128)(2,1)} %broadcast_in_dim.41.x_ref), custom_call_target="tpu_custom_call" | custom-call | tf_op jit(solution)/shard_map/pallas_call | solution.py:63
  435.9 11.3 %subtract_convert_fusion = (bf16[80,32,576]{2,1,0:T(8,128)(2,1)S(1)}, bf16[80,32,576]{2,1,0:T(8,128)(2,1)S(1)}) fusion(bf16[80,576,192]{1,2,0:T(8,128)(2,1)} %param.12, bf16[80,32,192]{2,1,0:T(8,128)(2,1)S(1)} %gather_fusion.7, pred[80]{0:T(512)(128)(4,1)S(1)} %compare_and_fusion), kind=kOutput, calls=%fused_computation.8 | convolution fusion | flops 572620800 | bytes 24576080 | tf_op jit(solution)/shard_map/tpl,tcl->tpc/dot_general | solution.py:136
  450.1 3.9 fusion.39.x_ref
  454.0 24.5 %shard_map.79 = bf16[32,1,32,576]{3,2,1,0:T(8,128)(2,1)} custom-call(bf16[32,1,32,576]{3,2,1,0:T(8,128)(2,1)} %fusion.39.x_ref), custom_call_target="tpu_custom_call" | custom-call | tf_op jit(solution)/shard_map/pallas_call | solution.py:63
  (63 shorter events, 64.5 us)
Async XLA Ops:
  0.0 2.7 copy-start
  35.1 11.7 %copy-start.3 = (s32[80]{0:T(128)S(1)}, s32[80]{0:T(128)}, u32[]{:S(2)}) copy-start(s32[80]{0:T(128)} %param.15) | copy-start | bytes 964
  81.3 11.3 %copy-start.2 = (s32[80]{0:T(128)S(1)}, s32[80]{0:T(128)}, u32[]{:S(2)}) copy-start(s32[80]{0:T(128)} %param.14) | copy-start | bytes 964
  454.0 26.0 %copy-start.1 = (f32[32,576]{1,0:T(8,128)S(1)}, f32[32,576]{1,0:T(8,128)}, u32[]{:S(2)}) copy-start(f32[32,576]{1,0:T(8,128)} %get-tuple-element.24) | copy-start | bytes 221188
